TPU v7x, 256 devices: a whole 4x4x8 slice. The times are simulated.
256 devices in a mesh: seq: 64 (over y, z_hi, x, core), dp: 4 (over z_lo).
Axes of the slice: x: 4, y: 4, z: 8 (z_hi: 2, z_lo: 4; z = z_hi * 4 + z_lo), core: 2. Of those that a mesh axis runs over, the one named last changes fastest.
Arguments:
- query: bfloat16 [4, 8192, 2048], P('dp', 'seq'), may hold values from -6 to 6
- keys: bfloat16 [4, 8192, 512], P('dp', 'seq'), may hold values from -6 to 6
- values: bfloat16 [4, 8192, 512], P('dp', 'seq'), may hold values from -6 to 6
- out_grad: bfloat16 [4, 8192, 2048], P('dp', 'seq'), may hold values from -16 to 16
- normed_input: bfloat16 [4, 8192, 4096], P('dp', 'seq'), may hold values from -16 to 16
- q_start: int32 [8], P('dp'), may hold values from 2048 to 3071, as said below
- q_len: int32 [8], P('dp'), may hold values from 1 to 512, as said below
Outputs:
- q_grad: bfloat16 [4, 8192, 2048], P('dp', 'seq')
- k_grad: bfloat16 [4, 8192, 512], P('dp', 'seq')
- v_grad: bfloat16 [4, 8192, 512], P('dp', 'seq')
- kv_weight_grad: float32 [4096, 1024], P(('seq', 'dp'))
Inputs may be any that keep to these rules, and one draw needn't show every extreme that they name: `q_start`: the visual part of each sequence ends here. `q_len`: tokens after the question are padding.
All inputs are finite; a program needn't handle non-finite values.
Results may differ from a plain program's by a relative error of at most 0.013.
Values may be sent and summed in bfloat16 or wider, within the bound.
A program may use at most 128 MiB of HBM per device.

v0:
```python
import math
import jax
import jax.numpy as jnp
from jax import lax
from jax.sharding import PartitionSpec as P

HEADS = 16
KV_HEADS = 4
HEAD_DIM = 128


def local(query, keys, values, out_grad, normed_input, q_start, q_len):
    seq_count = lax.axis_size("seq")
    tokens_dev = query.shape[1]
    repeat_by = HEADS // KV_HEADS
    classes = max(1, seq_count // HEADS)
    heads_dev = HEADS * classes // seq_count
    head_groups = seq_count // classes
    class_tokens = tokens_dev // classes
    seq_len = tokens_dev * seq_count // 2
    group_tokens = tokens_dev * seq_count
    width_dev = heads_dev * HEAD_DIM
    my_class = lax.axis_index("seq") // head_groups
    score_scale = 1.0 / math.sqrt(HEAD_DIM)

    def to_units(array):
        return array.reshape(class_tokens, seq_count, width_dev)

    query_units = to_units(query[0])
    grad_units = to_units(out_grad[0])
    key_wide = jnp.repeat(
        keys[0].reshape(tokens_dev, KV_HEADS, HEAD_DIM), repeat_by, axis=1
    ).reshape(tokens_dev, HEADS * HEAD_DIM)
    value_wide = jnp.repeat(
        values[0].reshape(tokens_dev, KV_HEADS, HEAD_DIM), repeat_by, axis=1
    ).reshape(tokens_dev, HEADS * HEAD_DIM)
    wide_shape = (tokens_dev, classes, head_groups, width_dev)
    key_units = jnp.broadcast_to(
        key_wide.reshape(tokens_dev, 1, head_groups, width_dev), wide_shape
    ).reshape(tokens_dev, seq_count, width_dev)
    value_units = jnp.broadcast_to(
        value_wide.reshape(tokens_dev, 1, head_groups, width_dev), wide_shape
    ).reshape(tokens_dev, seq_count, width_dev)
    query_got, grad_got, key_got, value_got = (
        lax.all_to_all(query_units, "seq", split_axis=1, concat_axis=0, tiled=True),
        lax.all_to_all(grad_units, "seq", split_axis=1, concat_axis=0, tiled=True),
        lax.all_to_all(key_units, "seq", split_axis=1, concat_axis=0, tiled=True),
        lax.all_to_all(value_units, "seq", split_axis=1, concat_axis=0, tiled=True),
    )
    block_rows = min(512, seq_len // classes)
    blocks_seq = seq_len // classes // block_rows
    key_pos = jnp.arange(seq_len, dtype=jnp.int32)

    def one_block(block_idx, carry):
        query_acc, key_acc, value_acc = carry
        seq_idx = block_idx // blocks_seq
        first_row = block_idx * block_rows
        key_first = seq_idx * seq_len
        query_block = lax.dynamic_slice_in_dim(query_got, first_row, block_rows, 0)
        grad_block = lax.dynamic_slice_in_dim(grad_got, first_row, block_rows, 0)
        key_block = lax.dynamic_slice_in_dim(key_got, key_first, seq_len, 0)
        value_block = lax.dynamic_slice_in_dim(value_got, key_first, seq_len, 0)
        start_pos = lax.dynamic_index_in_dim(q_start, seq_idx, 0, keepdims=False)
        end_pos = start_pos + lax.dynamic_index_in_dim(q_len, seq_idx, 0, keepdims=False)
        query_pos = (
            (first_row + jnp.arange(block_rows, dtype=jnp.int32)) * classes + my_class - key_first
        )
        visible = (key_pos[None, :] < end_pos) & (
            (key_pos[None, :] <= query_pos[:, None]) | (key_pos[None, :] < start_pos)
        )
        scores = (
            jnp.einsum("qhd,khd->hqk", query_block, key_block, preferred_element_type=jnp.float32)
            * score_scale
        )
        scores = jnp.where(visible[None], scores, -jnp.inf)
        row_max = jnp.max(scores, axis=-1, keepdims=True)
        exponent = jnp.where(visible[None], jnp.exp(scores - row_max), 0.0)
        probability = exponent / jnp.sum(exponent, axis=-1, keepdims=True)
        prob_low = probability.astype(jnp.bfloat16)
        dprob = jnp.einsum(
            "qhd,khd->hqk", grad_block, value_block, preferred_element_type=jnp.float32
        )
        row_delta = jnp.sum(probability * dprob, axis=-1, keepdims=True)
        dscore = (probability * (dprob - row_delta) * score_scale).astype(jnp.bfloat16)
        query_grad = jnp.einsum(
            "hqk,khd->qhd", dscore, key_block, preferred_element_type=jnp.float32
        ).astype(jnp.bfloat16)
        query_acc = lax.dynamic_update_slice_in_dim(query_acc, query_grad, first_row, 0)
        key_part = lax.dynamic_slice_in_dim(key_acc, key_first, seq_len, 0) + jnp.einsum(
            "hqk,qhd->khd", dscore, query_block, preferred_element_type=jnp.float32
        )
        value_part = lax.dynamic_slice_in_dim(value_acc, key_first, seq_len, 0) + jnp.einsum(
            "hqk,qhd->khd", prob_low, grad_block, preferred_element_type=jnp.float32
        )
        key_acc = lax.dynamic_update_slice_in_dim(key_acc, key_part, key_first, 0)
        value_acc = lax.dynamic_update_slice_in_dim(value_acc, value_part, key_first, 0)
        return (query_acc, key_acc, value_acc)

    start_state = (
        jnp.zeros((seq_count * class_tokens, heads_dev, HEAD_DIM), jnp.bfloat16),
        jnp.zeros((group_tokens, heads_dev, HEAD_DIM), jnp.float32),
        jnp.zeros((group_tokens, heads_dev, HEAD_DIM), jnp.float32),
    )
    query_acc, key_acc, value_acc = lax.fori_loop(0, 2 * blocks_seq, one_block, start_state)
    query_back = lax.all_to_all(
        query_acc.reshape(seq_count, class_tokens, 1, width_dev),
        "seq",
        split_axis=0,
        concat_axis=2,
        tiled=True,
    )
    query_grad_out = query_back.reshape(tokens_dev, HEADS * HEAD_DIM)
    key_back, value_back = (
        lax.all_to_all(
            key_acc.reshape(seq_count, tokens_dev, 1, width_dev).astype(jnp.bfloat16),
            "seq",
            split_axis=0,
            concat_axis=2,
            tiled=True,
        ).astype(jnp.float32),
        lax.all_to_all(
            value_acc.reshape(seq_count, tokens_dev, 1, width_dev).astype(jnp.bfloat16),
            "seq",
            split_axis=0,
            concat_axis=2,
            tiled=True,
        ).astype(jnp.float32),
    )
    key_grad_out = (
        key_back.reshape(tokens_dev, classes, KV_HEADS, repeat_by, HEAD_DIM)
        .sum(axis=(1, 3))
        .astype(jnp.bfloat16)
        .reshape(tokens_dev, KV_HEADS * HEAD_DIM)
    )
    value_grad_out = (
        value_back.reshape(tokens_dev, classes, KV_HEADS, repeat_by, HEAD_DIM)
        .sum(axis=(1, 3))
        .astype(jnp.bfloat16)
        .reshape(tokens_dev, KV_HEADS * HEAD_DIM)
    )
    joined = jnp.concatenate([key_grad_out, value_grad_out], axis=1)
    hidden_rows = normed_input[0]
    weight_out = lax.psum_scatter(
        jnp.einsum("tr,tc->rc", hidden_rows, joined, preferred_element_type=jnp.float32),
        ("seq", "dp"),
        scatter_dimension=0,
        tiled=True,
    )
    return (query_grad_out[None], key_grad_out[None], value_grad_out[None], weight_out)


def solution(mesh):
    in_specs = (
        P("dp", "seq", None),
        P("dp", "seq", None),
        P("dp", "seq", None),
        P("dp", "seq", None),
        P("dp", "seq", None),
        P("dp"),
        P("dp"),
    )
    out_specs = (
        P("dp", "seq", None),
        P("dp", "seq", None),
        P("dp", "seq", None),
        P(("seq", "dp"), None),
    )
    return jax.shard_map(local, mesh=mesh, in_specs=in_specs, out_specs=out_specs, check_vma=False)
```

profile of v0, /device:TPU:0, one launch (start us, length us, event | category | flops | bytes accessed | tf_op | source)
XLA Modules:
  0.0 1879.8 jit_solution(11580417287337845989)
XLA Ops:
  9.7 12.8 all-to-all-start.2
  25.0 15.2 all-to-all-done.2
  40.2 4.6 all-to-all-start.1
  45.0 16.3 all-to-all-done.1
  63.3 8.7 all-to-all-start.3
  72.1 32.6 %all-to-all-done.3 = bf16[128,64,128]{2,0,1:T(8,128)(2,1)} async-done(((bf16[128,64,128]{2,0,1:T(8,128)(2,1)}), bf16[128,64,128]{2,0,1:T(8,128)(2,1)}, u32[]{:S(2)}, u32[]{:S(2)}) %all-to-all-start.3) | async-done | bytes 2097184 | tf_op jit(solution)/shard_map/all_to_all | solution.py:48
  106.7 25.7 %all-to-all-start = ((bf16[128,64,128]{2,0,1:T(8,128)(2,1)}), bf16[128,64,128]{2,0,1:T(8,128)(2,1)S(1)}, u32[]{:S(2)}, u32[]{:S(2)}) async-start(bf16[128,64,128]{2,0,1:T(8,128)(2,1)} %bitcast.133), calls=%async_computation | async-start | bytes 4194304 | tf_op jit(solution)/shard_map/all_to_all | solution.py:47
  132.4 32.8 %all-to-all-done = bf16[128,64,128]{2,0,1:T(8,128)(2,1)S(1)} async-done(((bf16[128,64,128]{2,0,1:T(8,128)(2,1)}), bf16[128,64,128]{2,0,1:T(8,128)(2,1)S(1)}, u32[]{:S(2)}, u32[]{:S(2)}) %all-to-all-start) | async-done | bytes 2097184 | tf_op jit(solution)/shard_map/all_to_all | solution.py:47
  170.6 244.7 %while.21 = (s32[]{:T(128)}, bf16[2048,1,128]{2,0,1:T(8,128)(2,1)}, f32[8192,1,128]{2,0,1:T(8,128)}, f32[8192,1,128]{2,0,1:T(8,128)}, bf16[8192,1,128]{2,0,1:T(8...) while((s32[]{:T(128)}, bf16[2048,1,128]{2,0,1:T(8,128)(2,1)}, ...), condition=%wide.region_4.5_spmd.clone.clone, body=%wide.region_0.4_spmd.clone.clone.sunk | while | flops 2746294784 | bytes 167959120 | solution.py:104
  173.8 3.8 fusion.57
  177.6 4.2 fusion.58
  181.9 9.4 multiply_reduce_fusion.2
  191.3 10.0 multiply_convert_fusion.2
  204.9 3.7 fusion.61
  210.4 3.1 constant_dynamic-slice_fusion.4
  215.4 5.5 fusion.60
  224.0 4.1 constant_dynamic-update-slice_fusion.6
  235.0 3.8 fusion.57
  238.8 4.2 fusion.58
  243.0 9.4 multiply_reduce_fusion.2
  252.5 10.0 multiply_convert_fusion.2
  266.1 3.7 fusion.61
  271.6 3.1 constant_dynamic-slice_fusion.4
  276.6 5.5 fusion.60
  285.2 4.1 constant_dynamic-update-slice_fusion.6
  296.1 3.8 fusion.57
  299.9 4.2 fusion.58
  304.2 9.4 multiply_reduce_fusion.2
  313.6 10.0 multiply_convert_fusion.2
  327.2 3.7 fusion.61
  337.7 5.5 fusion.60
  346.3 4.0 constant_dynamic-update-slice_fusion.6
  357.3 3.8 fusion.57
  361.1 4.2 fusion.58
  365.3 9.4 multiply_reduce_fusion.2
  374.8 10.0 multiply_convert_fusion.2
  388.4 3.7 fusion.61
  393.9 3.1 constant_dynamic-slice_fusion.4
  398.9 5.5 fusion.60
  407.5 4.0 constant_dynamic-update-slice_fusion.6
  420.5 20.8 %all-to-all-start.5 = ((bf16[64,128,1,128]{1,3,2,0:T(8,128)(2,1)}), bf16[64,128,1,128]{1,3,2,0:T(8,128)(2,1)}, u32[]{:S(2)}, u32[]{:S(2)}) async-start(bf16[64,128,1,128]{1,3,2,0:T(8,128)(2,1)} %copy.46), calls=%async_computation.5 | async-start | bytes 4194304 | tf_op jit(solution)/shard_map/all_to_all | solution.py:114
  446.6 27.3 %all-to-all-done.5 = bf16[64,128,1,128]{1,3,2,0:T(8,128)(2,1)} async-done(((bf16[64,128,1,128]{1,3,2,0:T(8,128)(2,1)}), bf16[64,128,1,128]{1,3,2,0:T(8,128)(2,1)}, u32[]{:S(2)}, u32[]{:S(2)}) %all-to-all-start.5) | async-done | bytes 2097184 | tf_op jit(solution)/shard_map/all_to_all | solution.py:114
  474.0 25.7 %all-to-all-start.6 = ((bf16[64,128,1,128]{1,3,2,0:T(8,128)(2,1)}), bf16[64,128,1,128]{1,3,2,0:T(8,128)(2,1)S(1)}, u32[]{:S(2)}, u32[]{:S(2)}) async-start(bf16[64,128,1,128]{1,3,2,0:T(8,128)(2,1)} %copy.50), calls=%async_computation.6 | async-start | bytes 4194304 | tf_op jit(solution)/shard_map/all_to_all | solution.py:121
  501.7 30.9 %all-to-all-done.6 = bf16[64,128,1,128]{1,3,2,0:T(8,128)(2,1)S(1)} async-done(((bf16[64,128,1,128]{1,3,2,0:T(8,128)(2,1)}), bf16[64,128,1,128]{1,3,2,0:T(8,128)(2,1)S(1)}, u32[]{:S(2)}, u32[]{:S(2)}) %all-to-all-start.6) | async-done | bytes 2097184 | tf_op jit(solution)/shard_map/all_to_all | solution.py:121
  532.9 8.1 convolution_bitcast_fusion.2
  541.0 17.4 copy.58
  559.4 36.8 %all_to_all.105 = bf16[64,32,1,128]{3,1,2,0:T(8,128)(2,1)S(1)} all-to-all(bf16[64,32,1,128]{3,1,2,0:T(8,128)(2,1)S(1)} %bitcast.139), channel_id=1, replica_groups=mesh['seq'=64,'dp'=4] {'seq'}, dimensions={0} | all-to-all | bytes 1048576 | tf_op jit(solution)/shard_map/all_to_all | solution.py:105
  599.0 1274.0 %reduce-scatter.4.cloned.1.call-done = f32[16,1024]{1,0:T(8,128)} async-done(((f32[4096,1024]{1,0:T(8,128)}), f32[16,1024]{1,0:T(8,128)}) %reduce-scatter.4.cloned.1.call-update) | async-done | bytes 65552
  (128 shorter events, 98.3 us)
Async XLA Ops:
  7.2 525.7 %copy-start = (bf16[1,128,4096]{2,1,0:T(8,128)(2,1)S(1)}, bf16[1,128,4096]{2,1,0:T(8,128)(2,1)}, u32[]{:S(2)}) copy-start(bf16[1,128,4096]{2,1,0:T(8,128)(2,1)} %param.13) | copy-start | bytes 3145732
  7.2 37.7 %copy-start.8 = (bf16[1,128,512]{2,1,0:T(8,128)(2,1)S(1)}, bf16[1,128,512]{2,1,0:T(8,128)(2,1)}, u32[]{:S(2)}) copy-start(bf16[1,128,512]{2,1,0:T(8,128)(2,1)} %param.11) | copy-start | bytes 393220
  9.7 30.5 %all-to-all-start.2 = ((bf16[32,64,128]{2,0,1:T(8,128)(2,1)}), bf16[32,64,128]{2,0,1:T(8,128)(2,1)S(1)}, u32[]{:S(2)}, u32[]{:S(2)}) async-start(bf16[32,64,128]{2,0,1:T(8,128)(2,1)} %copy.40), calls=%async_computation.2 | async-start | bytes 1048576 | tf_op jit(solution)/shard_map/all_to_all | solution.py:46
  40.2 23.1 %copy-start.5 = (bf16[32,64,128]{2,0,1:T(8,128)(2,1)}, bf16[32,64,128]{2,0,1:T(8,128)(2,1)S(1)}, u32[]{:S(2)}) copy-start(bf16[32,64,128]{2,0,1:T(8,128)(2,1)S(1)} %all-to-all-done.2) | copy-start | bytes 1572868
  40.2 21.1 %all-to-all-start.1 = ((bf16[32,64,128]{2,0,1:T(8,128)(2,1)}), bf16[32,64,128]{2,0,1:T(8,128)(2,1)S(1)}, u32[]{:S(2)}, u32[]{:S(2)}) async-start(bf16[32,64,128]{2,0,1:T(8,128)(2,1)} %copy.39), calls=%async_computation.1 | async-start | bytes 1048576 | tf_op jit(solution)/shard_map/all_to_all | solution.py:45
  44.9 27.1 %copy-start.9 = (bf16[1,128,512]{2,1,0:T(8,128)(2,1)S(1)}, bf16[1,128,512]{2,1,0:T(8,128)(2,1)}, u32[]{:S(2)}) copy-start(bf16[1,128,512]{2,1,0:T(8,128)(2,1)} %param.10) | copy-start | bytes 393220
  61.3 43.5 %copy-start.6 = (bf16[32,64,128]{2,0,1:T(8,128)(2,1)}, bf16[32,64,128]{2,0,1:T(8,128)(2,1)S(1)}, u32[]{:S(2)}) copy-start(bf16[32,64,128]{2,0,1:T(8,128)(2,1)S(1)} %all-to-all-done.1) | copy-start | bytes 1572868
  63.3 41.4 %all-to-all-start.3 = ((bf16[128,64,128]{2,0,1:T(8,128)(2,1)}), bf16[128,64,128]{2,0,1:T(8,128)(2,1)}, u32[]{:S(2)}, u32[]{:S(2)}) async-start(bf16[128,64,128]{2,0,1:T(8,128)(2,1)} %bitcast.12), calls=%async_computation.3 | async-start | bytes 4194304 | tf_op jit(solution)/shard_map/all_to_all | solution.py:48
  106.7 58.5 %all-to-all-start = ((bf16[128,64,128]{2,0,1:T(8,128)(2,1)}), bf16[128,64,128]{2,0,1:T(8,128)(2,1)S(1)}, u32[]{:S(2)}, u32[]{:S(2)}) async-start(bf16[128,64,128]{2,0,1:T(8,128)(2,1)} %bitcast.133), calls=%async_computation | async-start | bytes 4194304 | tf_op jit(solution)/shard_map/all_to_all | solution.py:47
  165.2 5.4 copy-start.10
  165.2 5.4 copy-start.11
  170.6 7.0 copy-start.3
  220.9 3.1 copy-start.2
  224.0 4.1 copy-start.1
  228.1 3.7 copy-start.4
  231.8 7.0 copy-start.3
  282.1 3.1 copy-start.2
  285.2 4.1 copy-start.1
  289.3 3.7 copy-start.4
  293.0 7.0 copy-start.3
  343.3 3.1 copy-start.2
  346.3 4.1 copy-start.1
  350.4 3.7 copy-start.4
  354.1 7.0 copy-start.3
  404.4 3.1 copy-start.2
  407.5 4.1 copy-start.1
  411.5 3.7 copy-start.4
  420.5 53.4 %all-to-all-start.5 = ((bf16[64,128,1,128]{1,3,2,0:T(8,128)(2,1)}), bf16[64,128,1,128]{1,3,2,0:T(8,128)(2,1)}, u32[]{:S(2)}, u32[]{:S(2)}) async-start(bf16[64,128,1,128]{1,3,2,0:T(8,128)(2,1)} %copy.46), calls=%async_computation.5 | async-start | bytes 4194304 | tf_op jit(solution)/shard_map/all_to_all | solution.py:114
  474.0 58.6 %all-to-all-start.6 = ((bf16[64,128,1,128]{1,3,2,0:T(8,128)(2,1)}), bf16[64,128,1,128]{1,3,2,0:T(8,128)(2,1)S(1)}, u32[]{:S(2)}, u32[]{:S(2)}) async-start(bf16[64,128,1,128]{1,3,2,0:T(8,128)(2,1)} %copy.50), calls=%async_computation.6 | async-start | bytes 4194304 | tf_op jit(solution)/shard_map/all_to_all | solution.py:121
  499.7 1373.3 %reduce-scatter.4.cloned.1.call-start = ((), (), s32[]{:S(2)}) async-start(), calls=%async_computation.8 | async-start | bytes 16842752
  558.4 1.0 copy-start.7
Sparse Core Ops, SparseCore 0:
  558.5 1314.3 reduce-scatter.3
where the time goes:
time: 1880 us
  waiting for transfers between devices  1430 us (76%)
  local copies, waits for them, and re-layouts  120 us (6%)
  matrix products  109 us (6%)
  starting transfers between devices  98.4 us (5%)
  other arithmetic  66.8 us (4%)
  blocking collectives  36.8 us (2%)
    unnamed x2, waiting for transfers between devices  1270 us
    convert_element_type x4, other arithmetic, one_block(): (probability * (dprob - row_delta) * score_scale).astype(jnp.bfloat16)  40.1 us
    dot_general x4, matrix products, one_block(): jnp.einsum('qhd,khd->hqk', grad_block, value_block, preferred_element_typ...  37.7 us
  transfers between devices with their start and end apart: 7, of which 7 were waited for; matrix products, arithmetic and copies ran while one was open for 1% of the time, Pallas kernels for 0%

commit v1 on v0

--- a/solution.py
+++ b/solution.py
@@ -7,6 +7,13 @@
 HEADS = 16
 KV_HEADS = 4
 HEAD_DIM = 128
+
+
+def trade_parts(array, axis, split, join):
+    count = lax.axis_size(axis)
+    blocks = jnp.stack(jnp.split(array, count, axis=split), axis=0)
+    blocks = lax.all_to_all(blocks, axis, split_axis=0, concat_axis=0)
+    return jnp.concatenate(blocks, axis=join)
 
 
 def local(query, keys, values, out_grad, normed_input, q_start, q_len):
@@ -45,7 +52,7 @@
         lax.all_to_all(query_units, "seq", split_axis=1, concat_axis=0, tiled=True),
         lax.all_to_all(grad_units, "seq", split_axis=1, concat_axis=0, tiled=True),
         lax.all_to_all(key_units, "seq", split_axis=1, concat_axis=0, tiled=True),
-        lax.all_to_all(value_units, "seq", split_axis=1, concat_axis=0, tiled=True),
+        trade_parts(value_units, "seq", 1, 0),
     )
     block_rows = min(512, seq_len // classes)
     blocks_seq = seq_len // classes // block_rows

time: 1880 us -> 1890 us (level)
  local copies, waits for them, and re-layouts: 120 us -> 159 us
  starting transfers between devices: 98.4 us -> 61.9 us
    unnamed x19 -> x80, local copies, waits for them, and re-layouts: 20 us -> 58.1 us
    unnamed x2, waiting for transfers between devices: 1270 us -> 1300 us
    all_to_all x1, starting transfers between devices: 25.7 us -> 5.08 us  [local(): lax.all_to_all(value_acc.reshape(seq_count, tokens_dev, 1, width_dev).ast...]
  transfers between devices with their start and end apart: 7 -> 7, of which waited for: 7 -> 6; matrix products, arithmetic and copies ran while one was open for 1% -> 3% of each run, Pallas kernels for 0% -> 0%
where the time goes in v1:
time: 1890 us; the launch traced here: 1880 us
  waiting for transfers between devices  1440 us (76%)
  local copies, waits for them, and re-layouts  159 us (8%)
  matrix products  107 us (6%)
  other arithmetic  66.8 us (4%)
  starting transfers between devices  61.9 us (3%)
  blocking collectives  25.7 us (1%)
    unnamed x2, waiting for transfers between devices  1300 us
    unnamed x80, local copies, waits for them, and re-layouts  58.1 us
    convert_element_type x4, other arithmetic, one_block(): (probability * (dprob - row_delta) * score_scale).astype(jnp.bfloat16)  40.1 us
    all_to_all x1, waiting for transfers between devices, local(): lax.all_to_all(value_acc.reshape(seq_count, tokens_dev, 1, width_dev).ast...  38.3 us
  transfers between devices with their start and end apart: 7, of which 6 were waited for; matrix products, arithmetic and copies ran while one was open for 3% of the time, Pallas kernels for 0%

profile of v1, /device:TPU:0, one launch (start us, length us, event | category | flops | bytes accessed | tf_op | source)
XLA Modules:
  0.0 1884.7 jit_solution(11210329596813361479)
XLA Ops:
  9.7 13.1 all-to-all-start.2
  63.5 12.9 all-to-all-start.1
  79.5 14.5 all-to-all-done.1
  93.9 4.7 all-to-all-start.3
  98.7 32.8 %all-to-all-done.3 = bf16[64,128,1,128]{3,1,2,0:T(8,128)(2,1)S(1)} async-done(((bf16[64,128,1,128]{3,1,2,0:T(8,128)(2,1)}), bf16[64,128,1,128]{3,1,2,0:T(8,128)(2,1)S(1)}, u32[]{:S(2)}, u32[]{:S(2)}) %all-to-all-start.3) | async-done | bytes 2097184 | tf_op jit(solution)/shard_map/all_to_all | solution.py:15
  133.5 20.5 %all-to-all-start = ((bf16[128,64,128]{2,0,1:T(8,128)(2,1)}), bf16[128,64,128]{2,0,1:T(8,128)(2,1)S(1)}, u32[]{:S(2)}, u32[]{:S(2)}) async-start(bf16[128,64,128]{2,0,1:T(8,128)(2,1)} %bitcast.385), calls=%async_computation | async-start | bytes 4194304 | tf_op jit(solution)/shard_map/all_to_all | solution.py:54
  154.0 32.8 %all-to-all-done = bf16[128,64,128]{2,0,1:T(8,128)(2,1)S(1)} async-done(((bf16[128,64,128]{2,0,1:T(8,128)(2,1)}), bf16[128,64,128]{2,0,1:T(8,128)(2,1)S(1)}, u32[]{:S(2)}, u32[]{:S(2)}) %all-to-all-start) | async-done | bytes 2097184 | tf_op jit(solution)/shard_map/all_to_all | solution.py:54
  192.1 242.2 %while.21 = (s32[]{:T(128)}, bf16[2048,1,128]{2,0,1:T(8,128)(2,1)}, f32[8192,1,128]{2,0,1:T(8,128)}, f32[8192,1,128]{2,0,1:T(8,128)}, bf16[8192,1,128]{2,0,1:T(8...) while((s32[]{:T(128)}, bf16[2048,1,128]{2,0,1:T(8,128)(2,1)}, ...), condition=%wide.region_4.5_spmd.clone.clone, body=%wide.region_0.4_spmd.clone.clone.sunk | while | flops 2746294784 | bytes 176347760 | solution.py:111
  195.4 3.8 fusion.57
  199.2 4.2 fusion.58
  203.4 8.8 multiply_reduce_fusion.2
  212.2 10.0 multiply_convert_fusion.2
  225.8 3.7 fusion.61
  231.4 3.1 constant_dynamic-slice_fusion.4
  236.3 5.5 fusion.60
  245.0 4.1 constant_dynamic-update-slice_fusion.70
  255.9 3.8 fusion.57
  259.7 4.2 fusion.58
  264.0 8.8 multiply_reduce_fusion.2
  272.8 10.0 multiply_convert_fusion.2
  286.4 3.7 fusion.61
  291.9 3.1 constant_dynamic-slice_fusion.4
  296.9 5.5 fusion.60
  305.5 4.1 constant_dynamic-update-slice_fusion.70
  316.5 3.8 fusion.57
  320.3 4.2 fusion.58
  324.6 8.8 multiply_reduce_fusion.2
  333.4 10.0 multiply_convert_fusion.2
  347.0 3.7 fusion.61
  352.5 3.1 constant_dynamic-slice_fusion.4
  357.5 5.5 fusion.60
  366.1 4.0 constant_dynamic-update-slice_fusion.70
  377.0 3.8 fusion.57
  380.8 4.2 fusion.58
  385.1 8.8 multiply_reduce_fusion.2
  393.9 10.0 multiply_convert_fusion.2
  407.5 3.7 fusion.61
  413.0 3.1 constant_dynamic-slice_fusion.4
  418.0 5.5 fusion.60
  426.6 4.0 constant_dynamic-update-slice_fusion.70
  439.6 5.6 all-to-all-start.5
  450.5 27.2 %all-to-all-done.5 = bf16[64,128,1,128]{1,3,2,0:T(8,128)(2,1)} async-done(((bf16[64,128,1,128]{1,3,2,0:T(8,128)(2,1)}), bf16[64,128,1,128]{1,3,2,0:T(8,128)(2,1)}, u32[]{:S(2)}, u32[]{:S(2)}) %all-to-all-start.5) | async-done | bytes 2097184 | tf_op jit(solution)/shard_map/all_to_all | solution.py:121
  477.7 5.1 all-to-all-start.6
  484.7 38.3 %all-to-all-done.6 = bf16[64,128,1,128]{1,3,2,0:T(8,128)(2,1)S(1)} async-done(((bf16[64,128,1,128]{1,3,2,0:T(8,128)(2,1)}), bf16[64,128,1,128]{1,3,2,0:T(8,128)(2,1)S(1)}, u32[]{:S(2)}, u32[]{:S(2)}) %all-to-all-start.6) | async-done | bytes 2097184 | tf_op jit(solution)/shard_map/all_to_all | solution.py:128
  523.4 8.1 convolution_bitcast_fusion.2
  531.5 17.4 copy.247
  550.0 25.7 %all_to_all.92 = bf16[64,32,1,128]{3,1,2,0:T(8,128)(2,1)S(1)} all-to-all(bf16[64,32,1,128]{3,1,2,0:T(8,128)(2,1)S(1)} %bitcast.454), channel_id=1, replica_groups=mesh['seq'=64,'dp'=4] {'seq'}, dimensions={0} | all-to-all | bytes 1048576 | tf_op jit(solution)/shard_map/all_to_all | solution.py:112
  578.4 1299.4 %reduce-scatter.4.cloned.1.call-done = f32[16,1024]{1,0:T(8,128)} async-done(((f32[4096,1024]{1,0:T(8,128)}), f32[16,1024]{1,0:T(8,128)}) %reduce-scatter.4.cloned.1.call-update) | async-done | bytes 65552
  (198 shorter events, 134.4 us)
Async XLA Ops:
  7.2 516.3 %copy-start = (bf16[1,128,4096]{2,1,0:T(8,128)(2,1)S(1)}, bf16[1,128,4096]{2,1,0:T(8,128)(2,1)}, u32[]{:S(2)}) copy-start(bf16[1,128,4096]{2,1,0:T(8,128)(2,1)} %param.13) | copy-start | bytes 3145732
  7.2 15.6 copy-start.8
  9.7 53.8 %all-to-all-start.2 = ((bf16[32,64,128]{2,0,1:T(8,128)(2,1)}), bf16[32,64,128]{2,0,1:T(8,128)(2,1)}, u32[]{:S(2)}, u32[]{:S(2)}) async-start(bf16[32,64,128]{2,0,1:T(8,128)(2,1)} %copy.229), calls=%async_computation.2 | async-start | bytes 1048576 | tf_op jit(solution)/shard_map/all_to_all | solution.py:53
  63.5 30.5 %all-to-all-start.1 = ((bf16[32,64,128]{2,0,1:T(8,128)(2,1)}), bf16[32,64,128]{2,0,1:T(8,128)(2,1)}, u32[]{:S(2)}, u32[]{:S(2)}) async-start(bf16[32,64,128]{2,0,1:T(8,128)(2,1)} %copy.228), calls=%async_computation.1 | async-start | bytes 1048576 | tf_op jit(solution)/shard_map/all_to_all | solution.py:52
  79.5 19.2 %copy-start.9 = (bf16[1,128,512]{2,1,0:T(8,128)(2,1)S(1)}, bf16[1,128,512]{2,1,0:T(8,128)(2,1)}, u32[]{:S(2)}) copy-start(bf16[1,128,512]{2,1,0:T(8,128)(2,1)} %param.10) | copy-start | bytes 393220
  93.9 37.5 %all-to-all-start.3 = ((bf16[64,128,1,128]{3,1,2,0:T(8,128)(2,1)}), bf16[64,128,1,128]{3,1,2,0:T(8,128)(2,1)S(1)}, u32[]{:S(2)}, u32[]{:S(2)}) async-start(bf16[64,128,1,128]{3,1,2,0:T(8,128)(2,1)} %constant_dynamic-update-slice_fusion.3), calls=%async_computation.3 | async-start | bytes 4194304 | tf_op jit(solution)/shard_map/all_to_all | solution.py:15
  131.5 2.0 copy-start.5
  133.5 53.3 %all-to-all-start = ((bf16[128,64,128]{2,0,1:T(8,128)(2,1)}), bf16[128,64,128]{2,0,1:T(8,128)(2,1)S(1)}, u32[]{:S(2)}, u32[]{:S(2)}) async-start(bf16[128,64,128]{2,0,1:T(8,128)(2,1)} %bitcast.385), calls=%async_computation | async-start | bytes 4194304 | tf_op jit(solution)/shard_map/all_to_all | solution.py:54
  189.0 3.1 copy-start.10
  189.0 3.1 copy-start.11
  192.2 7.0 copy-start.3
  199.2 4.3 copy-start.6
  241.9 3.1 copy-start.2
  244.9 4.1 copy-start.1
  249.0 3.7 copy-start.4
  252.7 7.0 copy-start.3
  259.7 4.3 copy-start.6
  302.5 3.1 copy-start.2
  305.5 4.1 copy-start.1
  309.6 3.7 copy-start.4
  313.3 7.0 copy-start.3
  320.3 4.3 copy-start.6
  363.0 3.1 copy-start.2
  366.1 4.0 copy-start.1
  370.1 3.7 copy-start.4
  373.8 7.0 copy-start.3
  380.8 4.3 copy-start.6
  423.5 3.1 copy-start.2
  426.6 4.0 copy-start.1
  430.7 3.7 copy-start.4
  439.6 38.0 %all-to-all-start.5 = ((bf16[64,128,1,128]{1,3,2,0:T(8,128)(2,1)}), bf16[64,128,1,128]{1,3,2,0:T(8,128)(2,1)}, u32[]{:S(2)}, u32[]{:S(2)}) async-start(bf16[64,128,1,128]{1,3,2,0:T(8,128)(2,1)} %copy.235), calls=%async_computation.5 | async-start | bytes 4194304 | tf_op jit(solution)/shard_map/all_to_all | solution.py:121
  477.7 45.4 %all-to-all-start.6 = ((bf16[64,128,1,128]{1,3,2,0:T(8,128)(2,1)}), bf16[64,128,1,128]{1,3,2,0:T(8,128)(2,1)S(1)}, u32[]{:S(2)}, u32[]{:S(2)}) async-start(bf16[64,128,1,128]{1,3,2,0:T(8,128)(2,1)} %copy.239), calls=%async_computation.6 | async-start | bytes 4194304 | tf_op jit(solution)/shard_map/all_to_all | solution.py:128
  482.7 1395.1 %reduce-scatter.4.cloned.1.call-start = ((), (), s32[]{:S(2)}) async-start(), calls=%async_computation.8 | async-start | bytes 16842752
  548.9 1.0 copy-start.7
Sparse Core Ops, SparseCore 0:
  549.1 1328.7 reduce-scatter.3
